TPU v7x, 32 devices: a whole 2x2x4 slice. The times are simulated.
32 devices in a mesh: tm: 8 (over y, x, core), batch: 4 (over z).
Axes of the slice: x: 2, y: 2, z: 4, core: 2. Of those that a mesh axis runs over, the one named last changes fastest.
Arguments:
- hidden_states: bfloat16 [4, 1024, 5120], P('batch', 'tm'), may hold values from -6 to 6
- gen_weight: bfloat16 [64, 5120], replicated, may hold values from -0.078125 to 0.078125
- noise_field: bfloat16 [4, 64, 1024], P('batch', None, 'tm'), may hold values from -6 to 6
- timesteps: int32 [4], P('batch'), may hold values from 200 to 999
- embed_real: bfloat16 [128, 5120], replicated, may hold values from -0.5 to 0.5
- time_real: bfloat16 [256, 3, 5120], P('tm'), may hold values from -0.375 to 0.375
- query_real: bfloat16 [5120, 1024], P(None, 'tm'), may hold values from -3 to 3
- key_real: bfloat16 [5120, 1024], P(None, 'tm'), may hold values from -3 to 3
- value_real: bfloat16 [5120, 1024], P(None, 'tm'), may hold values from -0.078125 to 0.078125
- out_real: bfloat16 [1024, 5120], P('tm'), may hold values from -0.1875 to 0.1875
- gain_real: float32 [2, 1024], P(None, 'tm'), may hold values from 0.25 to 3
- proj_real: bfloat16 [64, 5120], replicated, may hold values from -0.078125 to 0.078125
- embed_fake: bfloat16 [128, 5120], replicated, may hold values from -0.5 to 0.5
- time_fake: bfloat16 [256, 3, 5120], P('tm'), may hold values from -0.375 to 0.375
- query_fake: bfloat16 [5120, 1024], P(None, 'tm'), may hold values from -3 to 3
- key_fake: bfloat16 [5120, 1024], P(None, 'tm'), may hold values from -3 to 3
- value_fake: bfloat16 [5120, 1024], P(None, 'tm'), may hold values from -0.078125 to 0.078125
- out_fake: bfloat16 [1024, 5120], P('tm'), may hold values from -0.1875 to 0.1875
- gain_fake: float32 [2, 1024], P(None, 'tm'), may hold values from 0.25 to 3
- proj_fake: bfloat16 [64, 5120], replicated, may hold values from -0.078125 to 0.078125
Outputs:
- dmd_gradient: float32 [4, 64, 1024], P('batch', None, 'tm')
- weight_grad: float32 [64, 5120], replicated
All inputs are finite; a program needn't handle non-finite values.
Results may differ from a plain program's by a relative error of at most 0.019.
Values may be sent and summed in bfloat16 or wider, within the bound.
No kernel may reach another device: no remote copies, remote signals or barrier semaphores. Data moves between devices by JAX's collectives and lax.ppermute only.
A program may use at most 128 MiB of HBM per device.

v0:
```python
import math

import jax
import jax.numpy as jnp
from jax import lax
from jax.sharding import PartitionSpec as P

HD = 128
FREQ = 256
FTOK = 128


norm_floor = 0.05
gap_floor = 0.25
highest = lax.Precision.HIGHEST


def from_behind(shard, axis, by):
    size = lax.axis_size(axis)
    pairs = [(i, i + by) for i in range(size) if 0 <= i + by < size]
    return lax.ppermute(shard, axis, pairs)


def sinusoid(time_step):
    half_freq = FREQ // 2
    frequency = jnp.exp(-math.log(10000.0) * jnp.arange(half_freq, dtype=jnp.float32) / half_freq)
    angles = time_step.astype(jnp.float32) * frequency
    return jnp.concatenate([jnp.cos(angles), jnp.sin(angles)]).astype(jnp.bfloat16)


def embed_stats(stacked, embed_table):
    embedded = lax.dot_general(
        stacked, embed_table, (((0,), (0,)), ((), ())), preferred_element_type=jnp.float32
    )
    row_mean = jnp.mean(embedded, axis=1)
    centered = embedded - row_mean[:, None]
    rscale = lax.rsqrt(jnp.mean(centered * centered, axis=1) + norm_floor)
    return (embedded, row_mean, rscale)


def fold_heads(embed_table, modulation, query_proj, key_proj, value_proj):
    scale_row = 1.0 + modulation[1]
    widened = embed_table.astype(jnp.float32) * scale_row[None, :]

    def fold_one(weight):
        wide_weight = weight.astype(jnp.float32)
        main_part = jnp.dot(widened, wide_weight, precision=highest)
        column_sum = jnp.dot(scale_row, wide_weight, precision=highest)
        offset = jnp.dot(modulation[0], wide_weight, precision=highest)
        return jnp.concatenate([main_part, column_sum[None, :], offset[None, :]], axis=0)

    return jnp.stack([fold_one(query_proj), fold_one(key_proj), fold_one(value_proj)])


def project(stacked, row_mean, rscale, folded):
    kin_rows = stacked.shape[0]
    base_part = jnp.einsum(
        "kr,pkc->prc", stacked.astype(jnp.float32), folded[:, :kin_rows], precision=highest
    )
    return (
        rscale[None, :, None] * base_part
        - (rscale * row_mean)[None, :, None] * folded[:, kin_rows][:, None, :]
        + folded[:, kin_rows + 1][:, None, :]
    )


def rms_round(vector, total_sq, columns, gain_row):
    return (
        vector * lax.rsqrt(total_sq / columns + norm_floor)[:, None] * gain_row[None, :]
    ).astype(jnp.bfloat16)


def attend(query_norm, key_norm, value_norm):
    token_count = query_norm.shape[0]
    block_rows = min(512, token_count)
    frames = jnp.arange(token_count, dtype=jnp.int32) // FTOK

    def one_block(row_start):
        query_block = lax.dynamic_slice_in_dim(query_norm, row_start, block_rows, 0)
        scores = jnp.einsum(
            "qhd,khd->hqk", query_block, key_norm, preferred_element_type=jnp.float32
        ) / math.sqrt(HD)
        query_frames = lax.dynamic_slice_in_dim(frames, row_start, block_rows, 0)
        allowed = frames[None, :] <= query_frames[:, None]
        scores = jnp.where(allowed[None], scores, -1e30)
        row_peak = jnp.max(scores, axis=2, keepdims=True)
        exp_scores = jnp.exp(scores - row_peak)
        attn_probs = (exp_scores / jnp.sum(exp_scores, axis=2, keepdims=True)).astype(jnp.bfloat16)
        return jnp.einsum(
            "hqk,khd->qhd", attn_probs, value_norm, preferred_element_type=jnp.float32
        ).astype(jnp.bfloat16)

    starts = jnp.arange(token_count // block_rows, dtype=jnp.int32) * block_rows
    pieces = lax.map(one_block, starts)
    return pieces.reshape(token_count, query_norm.shape[1], query_norm.shape[2])


def head_terms(attended, out_rows, modulation, final_proj):
    gated = out_rows.astype(jnp.float32) * modulation[2][None, :]
    folded_out = lax.dot_general(
        gated, final_proj.astype(jnp.float32), (((1,), (1,)), ((), ())), precision=highest
    )
    flat_heads = attended.reshape(attended.shape[0], -1).astype(jnp.float32)
    return lax.dot_general(folded_out, flat_heads, (((0,), (1,)), ((), ())), precision=highest)


def per_device(
    hidden_states,
    gen_weight,
    noise_field,
    timesteps,
    embed_real,
    time_real,
    query_real,
    key_real,
    value_real,
    out_real,
    gain_real,
    proj_real,
    embed_fake,
    time_fake,
    query_fake,
    key_fake,
    value_fake,
    out_fake,
    gain_fake,
    proj_fake,
):
    devices = lax.axis_size("tm")
    frame_tokens = hidden_states.shape[1]
    tokens = frame_tokens * devices
    patch_rows = gen_weight.shape[0]
    time_step = timesteps[0]
    level_raw = time_step.astype(jnp.float32) / 1000.0
    noise_level = 5.0 * level_raw / (1.0 + 4.0 * level_raw)
    generated = lax.dot_general(
        gen_weight, hidden_states[0], (((1,), (1,)), ((), ())), preferred_element_type=jnp.float32
    ).astype(jnp.bfloat16)
    noisy_patch = (
        (1.0 - noise_level) * generated.astype(jnp.float32)
        + noise_level * noise_field[0].astype(jnp.float32)
    ).astype(jnp.bfloat16)
    sinus_wave = sinusoid(time_step)
    freq_rows = time_real.shape[0]
    own_wave = lax.dynamic_slice_in_dim(sinus_wave, lax.axis_index("tm") * freq_rows, freq_rows, 0)
    share_real = jnp.einsum("f,fcd->cd", own_wave, time_real, preferred_element_type=jnp.float32)
    share_fake = jnp.einsum("f,fcd->cd", own_wave, time_fake, preferred_element_type=jnp.float32)
    modul_real, modul_fake = lax.psum((share_real, share_fake), "tm")
    earlier = from_behind(noisy_patch, "tm", 1)
    stacked = jnp.concatenate([noisy_patch, earlier], axis=0)
    embedded_real, mean_real, rscale_real = embed_stats(stacked, embed_real)
    embedded_fake, mean_fake, rscale_fake = embed_stats(stacked, embed_fake)
    folded_real = fold_heads(embed_real, modul_real, query_real, key_real, value_real)
    folded_fake = fold_heads(embed_fake, modul_fake, query_fake, key_fake, value_fake)
    local_width = query_real.shape[1]
    local_heads = local_width // HD
    columns = local_width * devices
    gathered = (
        lax.all_gather(noisy_patch.astype(jnp.float32), "tm", axis=1, tiled=True),
        lax.all_gather(mean_real, "tm", axis=0, tiled=True),
        lax.all_gather(rscale_real, "tm", axis=0, tiled=True),
        lax.all_gather(mean_fake, "tm", axis=0, tiled=True),
        lax.all_gather(rscale_fake, "tm", axis=0, tiled=True),
    )
    all_patch = gathered[0].astype(jnp.bfloat16)
    prior_frame = jnp.concatenate(
        [
            jnp.zeros((patch_rows, frame_tokens), jnp.bfloat16),
            all_patch[:, : tokens - frame_tokens],
        ],
        axis=1,
    )
    all_stacked = jnp.concatenate([all_patch, prior_frame], axis=0)
    qkv_real = project(all_stacked, gathered[1], gathered[2], folded_real)
    qkv_fake = project(all_stacked, gathered[3], gathered[4], folded_fake)
    norm_sums = lax.psum(
        (
            jnp.sum(qkv_real[0] * qkv_real[0], axis=1),
            jnp.sum(qkv_real[1] * qkv_real[1], axis=1),
            jnp.sum(qkv_fake[0] * qkv_fake[0], axis=1),
            jnp.sum(qkv_fake[1] * qkv_fake[1], axis=1),
        ),
        "tm",
    )
    head_shape = (tokens, local_heads, HD)
    attended_real = attend(
        rms_round(qkv_real[0], norm_sums[0], columns, gain_real[0]).reshape(head_shape),
        rms_round(qkv_real[1], norm_sums[1], columns, gain_real[1]).reshape(head_shape),
        qkv_real[2].astype(jnp.bfloat16).reshape(head_shape),
    )
    attended_fake = attend(
        rms_round(qkv_fake[0], norm_sums[2], columns, gain_fake[0]).reshape(head_shape),
        rms_round(qkv_fake[1], norm_sums[3], columns, gain_fake[1]).reshape(head_shape),
        qkv_fake[2].astype(jnp.bfloat16).reshape(head_shape),
    )
    term_real = head_terms(attended_real, out_real, modul_real, proj_real)
    term_fake = head_terms(attended_fake, out_fake, modul_fake, proj_fake)
    own_real, own_fake = (
        lax.psum_scatter(term_real, "tm", scatter_dimension=1, tiled=True),
        lax.psum_scatter(term_fake, "tm", scatter_dimension=1, tiled=True),
    )
    velocity_real = own_real + lax.dot_general(
        proj_real.astype(jnp.float32), embedded_real, (((1,), (1,)), ((), ())), precision=highest
    )
    velocity_fake = own_fake + lax.dot_general(
        proj_fake.astype(jnp.float32), embedded_fake, (((1,), (1,)), ((), ())), precision=highest
    )
    pred_real = noisy_patch.astype(jnp.float32) - noise_level * velocity_real
    pred_fake = noisy_patch.astype(jnp.float32) - noise_level * velocity_fake
    gap_local = jnp.sum(jnp.abs(generated.astype(jnp.float32) - pred_real))
    count_all = patch_rows * tokens
    grad_root = math.sqrt(lax.axis_size("batch") * hidden_states.shape[0] * tokens)
    gap_diff = pred_fake - pred_real
    difference = gap_diff.astype(jnp.bfloat16)
    partial_grad = jnp.dot(difference, hidden_states[0], preferred_element_type=jnp.float32)
    gap_total = lax.psum(gap_local, "tm")
    normalizer = jnp.maximum(gap_total / count_all, gap_floor)
    weight_grad = lax.psum(partial_grad / normalizer / grad_root, ("tm", "batch"))
    dmd_gradient = (gap_diff / normalizer)[None]
    return (dmd_gradient, weight_grad)


def solution(mesh):
    in_specs = (
        P("batch", "tm", None),
        P(),
        P("batch", None, "tm"),
        P("batch"),
        P(),
        P("tm", None, None),
        P(None, "tm"),
        P(None, "tm"),
        P(None, "tm"),
        P("tm", None),
        P(None, "tm"),
        P(),
        P(),
        P("tm", None, None),
        P(None, "tm"),
        P(None, "tm"),
        P(None, "tm"),
        P("tm", None),
        P(None, "tm"),
        P(),
    )
    out_specs = (P("batch", None, "tm"), P())
    return jax.shard_map(
        per_device, mesh=mesh, in_specs=in_specs, out_specs=out_specs, check_vma=False
    )
```

profile of v0, /device:TPU:0, one launch (start us, length us, event | category | flops | bytes accessed | tf_op | source)
XLA Modules:
  0.0 419.4 jit_solution(4317178082355693844)
XLA Ops:
  8.5 2.4 fusion.74
  10.9 2.4 collective-permute-start
  14.4 1.5 fusion.99
  16.0 25.7 %psum.59 = f32[3,5120]{1,0:T(4,128)S(1)} all-reduce(f32[3,5120]{1,0:T(4,128)S(1)} %bitcast.296), channel_id=1, replica_groups=mesh['tm'=8,'batch'=4] {'tm'}, use_global_device_ids=true, to_apply=%region_12.0 | all-reduce | flops 15360 | bytes 122880 | tf_op jit(solution)/shard_map/psum | solution.py:148
  46.3 1.5 fusion.18
  49.0 1.5 fusion.19
  52.7 1.5 fusion.101
  54.8 3.7 fusion.20
  58.5 10.2 %all_gather.16 = bf16[64,1024]{1,0:T(8,128)(2,1)S(1)} all-gather(bf16[64,128]{1,0:T(8,128)(2,1)S(1)} %get-tuple-element.224), channel_id=1, replica_groups=mesh['tm'=8,'batch'=4] {'tm'}, dimensions={1}, use_global_device_ids=true | all-gather | bytes 147456 | tf_op jit(solution)/shard_map/all_gather | solution.py:159
  70.5 7.6 %all-gather.2 = f32[8,1,128]{2,1,0:T(1,128)S(1)} all-gather(f32[1,1,128]{2,1,0:T(1,128)S(1)} %rsqrt_bitcast_fusion), channel_id=1, replica_groups=mesh['tm'=8,'batch'=4] {'tm'}, dimensions={0}, use_global_device_ids=true | all-gather | bytes 4608 | tf_op jit(solution)/shard_map/all_gather | solution.py:161
  78.1 9.0 %all-gather.3 = f32[8,1,128]{2,1,0:T(1,128)S(1)} all-gather(f32[1,1,128]{2,1,0:T(1,128)S(1)} %get-tuple-element.222), channel_id=1, replica_groups=mesh['tm'=8,'batch'=4] {'tm'}, dimensions={0}, use_global_device_ids=true | all-gather | bytes 4608 | tf_op jit(solution)/shard_map/all_gather | solution.py:160
  94.5 7.9 %all-gather = f32[8,1,128]{2,1,0:T(1,128)S(1)} all-gather(f32[1,1,128]{2,1,0:T(1,128)} %rsqrt_bitcast_fusion.1), channel_id=1, replica_groups=mesh['tm'=8,'batch'=4] {'tm'}, dimensions={0}, use_global_device_ids=true | all-gather | bytes 4608 | tf_op jit(solution)/shard_map/all_gather | solution.py:163
  102.4 8.7 %all-gather.1 = f32[8,1,128]{2,1,0:T(1,128)S(1)} all-gather(f32[1,1,128]{2,1,0:T(1,128)} %get-tuple-element.220), channel_id=1, replica_groups=mesh['tm'=8,'batch'=4] {'tm'}, dimensions={0}, use_global_device_ids=true | all-gather | bytes 4608 | tf_op jit(solution)/shard_map/all_gather | solution.py:162
  111.7 33.1 %all-reduce.8.cloned.1.call-done = (f32[1024]{0:T(1024)}, f32[1024]{0:T(1024)}, f32[3,5120]{1,0:T(4,128)}) async-done(((f32[1024]{0:T(1024)}, f32[1024]{0:T(1024)}, f32[3,5120]{1,0:T(4,128)}), (f32[1024]{0:T(1024)}, f32[1024]{0:T(1024)}, f32[3,5120]{1,0:T(4,128)})) %all-reduce.8.cloned.1.call-update) | async-done | bytes 69648 | tf_op jit(solution)/shard_map/psum | solution.py:176
  144.8 1.7 slice_add_fusion.1
  146.5 2.0 fusion.93
  148.4 2.0 fusion.83
  153.3 1.5 fusion.24
  158.9 9.1 %while.23 = (s32[]{:T(128)}, bf16[2,512,1,128]{3,1,2,0:T(8,128)(2,1)S(1)}, s32[1024]{0:T(1024)S(1)}, s32[2]{0:T(128)S(1)}, bf16[1024,1,128]{0,2,1:T(8,128)(2,1)S...) while((s32[]{:T(128)}, ...), condition=%wide.region_22.23_spmd.clone, body=%wide.region_19.22_spmd.clone.sunk | while | flops 273218560 | bytes 7098535 | solution.py:94
  169.4 2.1 fusion.30
  172.2 1.8 copy.41
  174.7 3.9 fusion.26
  178.6 25.1 %reduce-scatter.5.cloned.1.call-done = f32[64,128]{1,0:T(8,128)} async-done(((f32[64,1024]{1,0:T(8,128)}), f32[64,128]{1,0:T(8,128)}) %reduce-scatter.5.cloned.1.call-update) | async-done | bytes 32784 | tf_op jit(solution)/shard_map/reduce_scatter | solution.py:199
  203.6 4.6 %abs_reduce_fusion = (f32[]{:T(128)}, f32[64,128]{1,0:T(8,128)}) fusion(f32[64,128]{1,0:T(8,128)} %get-tuple-element.225, f32[64,128]{1,0:T(8,128)} %reduce-scatter.5.cloned.1.call-done, f32[128,5120]{1,0:T(8,128)} %copy-done.2, bf16[64,5120]{1,0:T(8,128)(2,1)S(1)} %copy-done.15, f32[]{:T(128)S(6)} %div.95, bf16[64,128]{1,0:T(8,128)(2,1)S(1)} %get-tuple-element.224), kind=kOutput, calls=%fused_computation.110 | convolution fusion | flops 503373824 | bytes 3391496 | tf_op jit(solution)/shard_map/dot_general | solution.py:202
  208.3 13.3 %all-reduce.1 = (f32[1024]{0:T(1024)S(1)}, f32[1024]{0:T(1024)S(1)}, f32[]{:T(128)}) all-reduce(f32[1024]{0:T(1024)} %get-tuple-element.163, f32[1024]{0:T(1024)} %get-tuple-element.162, f32[]{:T(128)} %get-tuple-element.230), channel_id=1, replica_groups=mesh['tm'=8,'batch'=4] {'tm'}, use_global_device_ids=true, to_apply=%region_4.0 | all-reduce | flops 2049 | bytes 16392 | tf_op jit(solution)/shard_map/psum | solution.py:176
  223.3 14.2 %while.22 = (s32[]{:T(128)}, bf16[2,512,1,128]{3,1,2,0:T(8,128)(2,1)S(1)}, s32[1024]{0:T(1024)}, s32[2]{0:T(128)}, bf16[1024,1,128]{0,2,1:T(8,128)(2,1)}, /*inde...) while((s32[]{:T(128)}, ...), condition=%wide.region_10.0_spmd.clone, body=%wide.region_7.10_spmd.clone.sunk | while | flops 273218560 | bytes 8147139 | solution.py:94
  227.2 1.7 fusion.163
  234.2 1.7 fusion.163
  239.3 33.3 %reduce-scatter.3.cloned.1.call-done = f32[64,128]{1,0:T(8,128)} async-done(((f32[64,1024]{1,0:T(8,128)}), f32[64,128]{1,0:T(8,128)}) %reduce-scatter.3.cloned.1.call-update) | async-done | bytes 32784 | tf_op jit(solution)/shard_map/reduce_scatter | solution.py:200
  272.6 3.4 fusion.46
  278.0 132.3 %all-reduce.6.cloned.1.call-done = f32[64,5120]{1,0:T(8,128)} async-done(((f32[64,5120]{1,0:T(8,128)}), f32[64,5120]{1,0:T(8,128)}) %all-reduce.6.cloned.1.call-update) | async-done | bytes 1310736 | tf_op jit(solution)/shard_map/psum | solution.py:218
  410.4 2.5 copy.87
  (168 shorter events, 46.5 us)
Async XLA Ops:
  7.2 1.3 copy-start
  7.2 137.6 %all-reduce.8.cloned.1.call-start = ((), (), s32[]{:S(2)}) async-start(), calls=%async_computation.5 | async-start | bytes 180224 | tf_op jit(solution)/shard_map/psum | solution.py:176
  8.5 33.3 %copy-start.5 = (bf16[5120,128]{1,0:T(8,128)(2,1)S(1)}, bf16[5120,128]{1,0:T(8,128)(2,1)}, u32[]{:S(2)}) copy-start(bf16[5120,128]{1,0:T(8,128)(2,1)} %param.32) | copy-start | bytes 3932164
  10.9 58.6 %collective-permute-start = (bf16[64,128]{1,0:T(8,128)(2,1)S(1)}, bf16[64,128]{1,0:T(8,128)(2,1)S(1)}, u32[]{:S(2)}, u32[]{:S(2)}) collective-permute-start(bf16[64,128]{1,0:T(8,128)(2,1)S(1)} %get-tuple-element.224), channel_id=1, source_target_pairs={{0,4},{4,8},{8,12},{12,16},{16,20},{20,24},{24,28},{1,5},{5,9},{9,... | collective-permute-start | bytes 49160 | tf_op jit(solution)/shard_map/ppermute | solution.py:21
  14.4 28.6 %copy-start.31 = (bf16[256]{0:T(256)(128)(2,1)}, bf16[256]{0:T(256)(128)(2,1)S(1)}, u32[]{:S(2)}) copy-start(bf16[256]{0:T(256)(128)(2,1)S(1)} %pad_maximum_fusion.9) | copy-start | bytes 1540
  43.0 1.7 copy-start.6
  46.3 1.5 copy-start.8
  50.6 3.6 copy-start.34
  50.6 4.2 %copy-start.15 = (bf16[64,5120]{1,0:T(8,128)(2,1)S(1)}, bf16[64,5120]{1,0:T(8,128)(2,1)}, u32[]{:S(2)}) copy-start(bf16[64,5120]{1,0:T(8,128)(2,1)} %param.35) | copy-start | bytes 1966084
  68.7 18.4 %copy-start.17 = (bf16[64,1024]{1,0:T(8,128)(2,1)}, bf16[64,1024]{1,0:T(8,128)(2,1)S(1)}, u32[]{:S(2)}) copy-start(bf16[64,1024]{1,0:T(8,128)(2,1)S(1)} %all_gather.16) | copy-start | bytes 393220
  68.7 18.4 %copy-start.25 = (bf16[64,896]{1,0:T(8,128)(2,1)}, bf16[64,896]{1,0:T(8,128)(2,1)S(1)}, u32[]{:S(2)}) copy-start(bf16[64,896]{1,0:T(8,128)(2,1)S(1)} %slice.122) | copy-start | bytes 344068
  70.1 18.1 %copy-start.2 = (f32[128,5120]{1,0:T(8,128)}, f32[128,5120]{1,0:T(8,128)S(1)}, u32[]{:S(2)}) copy-start(f32[128,5120]{1,0:T(8,128)S(1)} %get-tuple-element.227) | copy-start | bytes 7864324
  70.1 17.0 %copy-start.20 = (f32[3,130,128]{2,1,0:T(8,128)S(1)}, f32[3,130,128]{2,1,0:T(8,128)}, u32[]{:S(2)}) copy-start(f32[3,130,128]{2,1,0:T(8,128)} %pad_maximum_fusion.1) | copy-start | bytes 599044
  87.1 2.2 copy-start.4
  87.1 2.2 copy-start.27
  90.0 1.5 copy-start.1
  92.4 111.2 %reduce-scatter.5.cloned.1.call-start = ((), (), s32[]{:S(2)}) async-start(), calls=%async_computation.3 | async-start | bytes 294912 | tf_op jit(solution)/shard_map/reduce_scatter | solution.py:199
  102.4 42.3 %copy-start.28 = (f32[8,1,128]{2,1,0:T(1,128)}, f32[8,1,128]{2,1,0:T(1,128)S(1)}, u32[]{:S(2)}) copy-start(f32[8,1,128]{2,1,0:T(1,128)S(1)} %all-gather) | copy-start | bytes 12292
  144.8 5.7 %copy-start.10 = (bf16[5120,128]{1,0:T(8,128)(2,1)S(1)}, bf16[5120,128]{1,0:T(8,128)(2,1)}, u32[]{:S(2)}) copy-start(bf16[5120,128]{1,0:T(8,128)(2,1)} %param.39) | copy-start | bytes 3932164
  144.8 5.7 %copy-start.14 = (f32[3,5120]{1,0:T(4,128)S(1)}, f32[3,5120]{1,0:T(4,128)}, u32[]{:S(2)}) copy-start(f32[3,5120]{1,0:T(4,128)} %get-tuple-element.199) | copy-start | bytes 184324
  153.3 1.5 copy-start.11
  156.1 2.4 copy-start.30
  156.1 2.4 copy-start.29
  156.1 2.4 copy-start.13
  156.1 2.4 copy-start.32
  156.1 2.4 copy-start.33
  158.9 9.1 %copy-start.23 = (f32[128,64]{0,1:T(8,128)S(1)}, f32[128,64]{0,1:T(8,128)}, u32[]{:S(2)}) copy-start(f32[128,64]{0,1:T(8,128)} %fusion.20) | copy-start | bytes 98308
  169.1 103.5 %reduce-scatter.3.cloned.1.call-start = ((), (), s32[]{:S(2)}) async-start(), calls=%async_computation.2 | async-start | bytes 294912 | tf_op jit(solution)/shard_map/reduce_scatter | solution.py:200
  223.3 14.2 %copy-start.24 = (f32[128,64]{0,1:T(8,128)S(1)}, f32[128,64]{0,1:T(8,128)}, u32[]{:S(2)}) copy-start(f32[128,64]{0,1:T(8,128)} %fusion.26) | copy-start | bytes 98308
  223.3 49.3 %copy-start.16 = (bf16[64,5120]{1,0:T(8,128)(2,1)S(1)}, bf16[64,5120]{1,0:T(8,128)(2,1)}, u32[]{:S(2)}) copy-start(bf16[64,5120]{1,0:T(8,128)(2,1)} %param.43) | copy-start | bytes 1966084
  223.3 49.3 %copy-start.22 = (f32[64,128]{1,0:T(8,128)S(1)}, f32[64,128]{1,0:T(8,128)}, u32[]{:S(2)}) copy-start(f32[64,128]{1,0:T(8,128)} %get-tuple-element.231) | copy-start | bytes 98308
  238.6 171.7 %all-reduce.6.cloned.1.call-start = ((), (), s32[]{:S(2)}) async-start(), calls=%async_computation.4 | async-start | bytes 2621440 | tf_op jit(solution)/shard_map/psum | solution.py:218
  (10 other events, 11.2 us)
Sparse Core Ops, SparseCore 0:
  92.6 52.1 all-reduce.7
  169.2 34.3 reduce-scatter.4
  238.7 33.7 reduce-scatter.2
  278.4 131.9 all-reduce.5
where the time goes:
time: 421 us; the launch traced here: 419 us
  waiting for transfers between devices  224 us (53%)
  blocking collectives  82.3 us (20%)
  matrix products  55.5 us (13%)
  local copies, waits for them, and re-layouts  17.6 us (4%)
  between operations  15.8 us (4%)
  other arithmetic  13.9 us (3%)
  loops' own time  7.68 us (2%)
    psum x1, waiting for transfers between devices, per_device(): lax.psum(partial_grad / normalizer / grad_root, ('tm', 'batch'))  132 us
    reduce_scatter x1, waiting for transfers between devices, per_device(): lax.psum_scatter(term_fake, 'tm', scatter_dimension=1, tiled=True)  33.3 us
    psum x1, waiting for transfers between devices, per_device(): lax.psum((jnp.sum(qkv_real[0] * qkv_real[0], axis=1), jnp.sum(qkv_real[1]...  33.1 us
    psum x1, blocking collectives, per_device(): modul_real, modul_fake = lax.psum((share_real, share_fake), 'tm')  25.7 us
    reduce_scatter x1, waiting for transfers between devices, per_device(): lax.psum_scatter(term_real, 'tm', scatter_dimension=1, tiled=True)  25.1 us
    psum x1, blocking collectives, per_device(): lax.psum((jnp.sum(qkv_real[0] * qkv_real[0], axis=1), jnp.sum(qkv_real[1]...  13.3 us
    all_gather x1, blocking collectives, per_device(): lax.all_gather(noisy_patch.astype(jnp.float32), 'tm', axis=1, tiled=True)  10.2 us
    dot_general x6, matrix products, fold_one(): main_part = jnp.dot(widened, wide_weight, precision=highest)  9.04 us
  transfers between devices with their start and end apart: 5, of which 4 were waited for; matrix products, arithmetic and copies ran while one was open for 8% of the time, Pallas kernels for 0%

commit v1 on v0

v1 whole, which is shorter than its diff:
```python
import math

import jax
import jax.numpy as jnp
from jax import lax
from jax.sharding import PartitionSpec as P

HD = 128
FREQ = 256
FTOK = 128


norm_floor = 0.05
gap_floor = 0.25


def sinusoid(time_step):
    half_freq = FREQ // 2
    frequency = jnp.exp(-math.log(10000.0) * jnp.arange(half_freq, dtype=jnp.float32) / half_freq)
    angles = time_step.astype(jnp.float32) * frequency
    return jnp.concatenate([jnp.cos(angles), jnp.sin(angles)]).astype(jnp.bfloat16)


def split_two(wide):
    top = lax.reduce_precision(wide, 8, 7)
    return top.astype(jnp.bfloat16), (wide - top).astype(jnp.bfloat16)


def dot32(left, right, left_dim, right_dim):
    return lax.dot_general(
        left, right, (((left_dim,), (right_dim,)), ((), ())), preferred_element_type=jnp.float32
    )


def centre(embed_table):
    wide = embed_table.astype(jnp.float32)
    return wide - jnp.mean(wide, axis=1, keepdims=True)


def gram_of(centered):
    top, low = split_two(centered)
    cross = dot32(top, low, 1, 1)
    return (dot32(top, top, 1, 1) + cross + cross.T) / centered.shape[1]


def fold_heads(centered, shift, scale, weights):
    rows = jnp.concatenate(
        [centered * (1.0 + scale)[None, :], jnp.broadcast_to(shift[None, :], (16, shift.shape[0]))]
    )
    count = rows.shape[0]
    both = jnp.concatenate(split_two(rows))
    folded = [dot32(both, weight, 1, 0) for weight in weights]
    folded = [piece[:count] + piece[count:] for piece in folded]
    kin_rows = centered.shape[0]
    main = jnp.concatenate([piece[:kin_rows] for piece in folded], axis=1)
    offset = jnp.concatenate([piece[kin_rows] for piece in folded])
    return main, offset


def project(token_rows, gram, main, offset):
    kin = token_rows.shape[1]
    table = jnp.concatenate(split_two(jnp.concatenate([main, gram], axis=1)))
    twice = jnp.concatenate([token_rows, token_rows], axis=1)
    product = dot32(twice, table, 1, 0)
    width = main.shape[1]
    variance = jnp.sum(product[:, width:] * token_rows.astype(jnp.float32), axis=1)
    rscale = lax.rsqrt(jnp.maximum(variance, 0.0) + norm_floor)
    return rscale[:, None] * product[:, :width] + offset[None, :]


def rms_round(vector, total_sq, columns, gain_row):
    return (
        vector * lax.rsqrt(total_sq / columns + norm_floor)[:, None] * gain_row[None, :]
    ).astype(jnp.bfloat16)


def attend(query_norm, key_norm, value_norm):
    tokens = query_norm.shape[1]
    block = min(256, tokens)
    frames = jnp.arange(tokens, dtype=jnp.int32) // FTOK
    pieces = []
    for start in range(0, tokens, block):
        stop = start + block
        scores = jnp.einsum(
            "hqd,hkd->hqk",
            query_norm[:, start:stop],
            key_norm[:, :stop],
            preferred_element_type=jnp.float32,
        ) / math.sqrt(HD)
        allowed = frames[None, :stop] <= frames[start:stop, None]
        scores = jnp.where(allowed[None], scores, -1e30)
        peak = jnp.max(scores, axis=2, keepdims=True)
        weights = jnp.exp(scores - peak)
        total = jnp.sum(weights, axis=2, keepdims=True)
        mixed = jnp.einsum(
            "hqk,hkd->hqd",
            weights.astype(jnp.bfloat16),
            value_norm[:, :stop],
            preferred_element_type=jnp.float32,
        )
        pieces.append((mixed / total).astype(jnp.bfloat16))
    return jnp.concatenate(pieces, axis=1)


def fold_out(out_rows, gate, final_proj):
    top, low = split_two(out_rows.astype(jnp.float32) * gate[None, :])
    return dot32(final_proj, top, 1, 1) + dot32(final_proj, low, 1, 1)


def per_device(
    hidden_states,
    gen_weight,
    noise_field,
    timesteps,
    embed_real,
    time_real,
    query_real,
    key_real,
    value_real,
    out_real,
    gain_real,
    proj_real,
    embed_fake,
    time_fake,
    query_fake,
    key_fake,
    value_fake,
    out_fake,
    gain_fake,
    proj_fake,
):
    devices = lax.axis_size("tm")
    samples = lax.axis_size("batch")
    place = lax.axis_index("tm")
    frame_tokens = hidden_states.shape[1]
    tokens = frame_tokens * devices
    patch_rows = gen_weight.shape[0]
    width = gen_weight.shape[1]
    time_step = timesteps[0]
    level_raw = time_step.astype(jnp.float32) / 1000.0
    noise_level = 5.0 * level_raw / (1.0 + 4.0 * level_raw)
    generated = dot32(gen_weight, hidden_states[0], 1, 1).astype(jnp.bfloat16)
    noisy_patch = (
        (1.0 - noise_level) * generated.astype(jnp.float32)
        + noise_level * noise_field[0].astype(jnp.float32)
    ).astype(jnp.bfloat16)
    sinus_wave = sinusoid(time_step)
    freq_rows = time_real.shape[0]
    own_wave = lax.dynamic_slice_in_dim(sinus_wave, place * freq_rows, freq_rows, 0)
    shares = [
        jnp.einsum("f,fcd->cd", own_wave, table, preferred_element_type=jnp.float32)
        for table in (time_real, time_fake)
    ]
    shares = jnp.concatenate(shares).astype(jnp.bfloat16)
    modul_rows = shares.shape[0]
    payload = jnp.concatenate([noisy_patch, shares.reshape(-1, frame_tokens)])
    gathered = lax.all_gather(payload, "tm", axis=0, tiled=False)
    modul = jnp.sum(gathered[:, patch_rows:].astype(jnp.float32), axis=0)
    modul = modul.reshape(modul_rows, width)
    modul_real, modul_fake = modul[:3], modul[3:]
    patches = gathered[:, :patch_rows]
    patch_tokens = jnp.transpose(patches, (0, 2, 1)).reshape(tokens, patch_rows)
    prior = jnp.concatenate(
        [
            jnp.zeros((frame_tokens, patch_rows), jnp.bfloat16),
            patch_tokens[: tokens - frame_tokens],
        ]
    )
    token_rows = jnp.concatenate([patch_tokens, prior], axis=1)
    own_rows = lax.dynamic_slice_in_dim(token_rows, place * frame_tokens, frame_tokens, 0)

    def one_network(embed_table, modulation, query, key, value):
        centered = centre(embed_table)
        main, offset = fold_heads(centered, modulation[0], modulation[1], (query, key, value))
        return project(token_rows, gram_of(centered), main, offset)

    qkv_real = one_network(embed_real, modul_real, query_real, key_real, value_real)
    qkv_fake = one_network(embed_fake, modul_fake, query_fake, key_fake, value_fake)
    local_width = query_real.shape[1]
    columns = local_width * devices

    def columns_of(stacked, part):
        return stacked[:, part * local_width : (part + 1) * local_width]

    vectors = [
        columns_of(qkv_real, 0),
        columns_of(qkv_real, 1),
        columns_of(qkv_fake, 0),
        columns_of(qkv_fake, 1),
    ]
    squares = jnp.stack([jnp.sum(vector * vector, axis=1) for vector in vectors])
    norm_sums = jnp.sum(lax.all_gather(squares, "tm", axis=0, tiled=False), axis=0)
    gains = [gain_real[0], gain_real[1], gain_fake[0], gain_fake[1]]
    normed = [
        rms_round(vector, norm_sums[i], columns, gains[i]) for i, vector in enumerate(vectors)
    ]
    local_heads = local_width // HD

    def heads_of(parts):
        pieces = [
            part[:, h * HD : (h + 1) * HD] for part in parts for h in range(local_heads)
        ]
        return jnp.stack(pieces)

    attended = attend(
        heads_of((normed[0], normed[2])),
        heads_of((normed[1], normed[3])),
        heads_of(
            (
                columns_of(qkv_real, 2).astype(jnp.bfloat16),
                columns_of(qkv_fake, 2).astype(jnp.bfloat16),
            )
        ),
    )

    def head_terms(pieces, out_rows, gate, final_proj):
        flat = jnp.concatenate([pieces[h] for h in range(local_heads)], axis=1)
        framed = flat.reshape(devices, frame_tokens, local_width)
        top, low = split_two(fold_out(out_rows, gate, final_proj))
        terms = [
            jnp.einsum("pd,jtd->jpt", part, framed, preferred_element_type=jnp.float32)
            for part in (top, low)
        ]
        return terms[0] + terms[1]

    term_real = head_terms(attended[:local_heads], out_real, modul_real[2], proj_real)
    term_fake = head_terms(attended[local_heads:], out_fake, modul_fake[2], proj_fake)
    sent = jnp.concatenate([term_real, term_fake - term_real], axis=1).astype(jnp.bfloat16)
    landed = lax.all_to_all(sent, "tm", 0, 0, tiled=True)
    own_terms = jnp.sum(landed.astype(jnp.float32), axis=0)

    def base_of(final_proj, embed_table):
        top, low = split_two(dot32(final_proj, embed_table, 1, 1))
        return dot32(top, own_rows, 1, 1) + dot32(low, own_rows, 1, 1)

    base_real = base_of(proj_real, embed_real)
    base_fake = base_of(proj_fake, embed_fake)
    velocity_real = own_terms[:patch_rows] + base_real
    velocity_diff = own_terms[patch_rows:] + (base_fake - base_real)
    pred_real = noisy_patch.astype(jnp.float32) - noise_level * velocity_real
    gap_local = jnp.sum(jnp.abs(generated.astype(jnp.float32) - pred_real))
    gap_diff = -noise_level * velocity_diff
    difference = gap_diff.astype(jnp.bfloat16)
    partial_grad = jnp.dot(difference, hidden_states[0], preferred_element_type=jnp.float32)
    everyone = devices * samples
    lanes = 128
    blocks = jnp.transpose(
        partial_grad.astype(jnp.bfloat16).reshape(patch_rows, width // lanes, lanes), (1, 0, 2)
    ).reshape(everyone, -1, lanes)
    chunk_rows = blocks.shape[1]
    gap_top, gap_low = split_two(gap_local)
    lane = lax.broadcasted_iota(jnp.int32, (everyone, 16, lanes), 2)
    gap_rows = jnp.where(lane == 0, gap_top, gap_low)
    traded = lax.all_to_all(
        jnp.concatenate([blocks, gap_rows], axis=1), ("tm", "batch"), 0, 0, tiled=True
    ).astype(jnp.float32)
    gaps = traded[:, chunk_rows, 0] + traded[:, chunk_rows, 1]
    gap_total = jnp.sum(gaps.reshape(devices, samples), axis=0)
    count_all = patch_rows * tokens
    normalizers = jnp.maximum(gap_total / count_all, gap_floor)
    grad_root = math.sqrt(samples * hidden_states.shape[0] * tokens)
    per_source = jnp.tile(1.0 / (normalizers * grad_root), devices)
    own_chunk = jnp.sum(traded[:, :chunk_rows] * per_source[:, None, None], axis=0)
    whole = lax.all_gather(own_chunk.astype(jnp.bfloat16), ("tm", "batch"), axis=0, tiled=True)
    weight_grad = (
        jnp.transpose(whole.reshape(width // lanes, patch_rows, lanes), (1, 0, 2))
        .reshape(patch_rows, width)
        .astype(jnp.float32)
    )
    own_norm = lax.dynamic_index_in_dim(normalizers, lax.axis_index("batch"), 0, keepdims=False)
    dmd_gradient = (gap_diff / own_norm)[None]
    return (dmd_gradient, weight_grad)


def solution(mesh):
    in_specs = (
        P("batch", "tm", None),
        P(),
        P("batch", None, "tm"),
        P("batch"),
        P(),
        P("tm", None, None),
        P(None, "tm"),
        P(None, "tm"),
        P(None, "tm"),
        P("tm", None),
        P(None, "tm"),
        P(),
        P(),
        P("tm", None, None),
        P(None, "tm"),
        P(None, "tm"),
        P(None, "tm"),
        P("tm", None),
        P(None, "tm"),
        P(),
    )
    out_specs = (P("batch", None, "tm"), P())
    return jax.shard_map(
        per_device, mesh=mesh, in_specs=in_specs, out_specs=out_specs, check_vma=False
    )
```

time: 421 us -> 188 us (0.45)
  waiting for transfers between devices: 224 us -> 23.6 us
  matrix products: 55.5 us -> 26.3 us
  blocking collectives: 82.3 us -> 92.8 us
  between operations: 15.8 us -> 5.66 us
  loops' own time: 7.68 us -> 0 us
  starting transfers between devices: 2.77 us -> 7.37 us
    psum x2 -> x0, waiting for transfers between devices: 165 us -> none  [the longest x1 132 us: per_device(): lax.psum(partial_grad / normalizer / grad_root, ('tm', 'batch'))]
    reduce_scatter x2 -> x0, waiting for transfers between devices: 58.3 us -> none  [the longest x1 33.3 us: per_device(): lax.psum_scatter(term_fake, 'tm', scatter_dimension=1, tiled=True)]
    all_gather x5 -> x3, blocking collectives: 43.4 us -> 92.8 us  [the longest x1 71.9 us: per_device(): lax.all_gather(own_chunk.astype(jnp.bfloat16), ('tm', 'batch'), axis=0, t...]
    psum x2 -> x0, blocking collectives: 39 us -> none  [the longest x1 25.7 us: per_device(): modul_real, modul_fake = lax.psum((share_real, share_fake), 'tm')]
    dot_general x39 -> x37, matrix products: 54.1 us -> 25.9 us  [the longest x23 18.2 us: dot32(): lax.dot_general(left, right, (((left_dim,), (right_dim,)), ((), ())), pre...]
    all_to_all x0 -> x2, waiting for transfers between devices: none -> 23.6 us  [the longest x1 19.5 us: per_device(): lax.all_to_all(jnp.concatenate([blocks, gap_rows], axis=1), ('tm', 'batch...]
    another operation x2 -> x0, loops' own time: 7.68 us -> none  [attend(): pieces = lax.map(one_block, starts)]
    all_to_all x0 -> x2, starting transfers between devices: none -> 7.37 us  [the longest x1 3.96 us: per_device(): lax.all_to_all(jnp.concatenate([blocks, gap_rows], axis=1), ('tm', 'batch...]
  transfers between devices with their start and end apart: 5 -> 2, of which waited for: 4 -> 2; matrix products, arithmetic and copies ran while one was open for 8% -> 1% of each run, Pallas kernels for 0% -> 0%
where the time goes in v1:
time: 188 us; the launch traced here: 187 us
  blocking collectives  92.8 us (49%)
  matrix products  26.3 us (14%)
  waiting for transfers between devices  23.6 us (13%)
  other arithmetic  17.4 us (9%)
  local copies, waits for them, and re-layouts  14 us (7%)
  starting transfers between devices  7.37 us (4%)
  between operations  5.66 us (3%)
    all_gather x1, blocking collectives, per_device(): lax.all_gather(own_chunk.astype(jnp.bfloat16), ('tm', 'batch'), axis=0, t...  71.9 us
    all_to_all x1, waiting for transfers between devices, per_device(): lax.all_to_all(jnp.concatenate([blocks, gap_rows], axis=1), ('tm', 'batch...  19.5 us
    dot_general x23, matrix products, dot32(): lax.dot_general(left, right, (((left_dim,), (right_dim,)), ((), ())), pre...  18.2 us
    all_gather x1, blocking collectives, per_device(): gathered = lax.all_gather(payload, 'tm', axis=0, tiled=False)  11.6 us
    unnamed x68, local copies, waits for them, and re-layouts  9.39 us
    all_gather x1, blocking collectives, per_device(): lax.all_gather(squares, 'tm', axis=0, tiled=False)  9.37 us
    all_to_all x1, waiting for transfers between devices, per_device(): landed = lax.all_to_all(sent, 'tm', 0, 0, tiled=True)  4.12 us
    all_to_all x1, starting transfers between devices, per_device(): lax.all_to_all(jnp.concatenate([blocks, gap_rows], axis=1), ('tm', 'batch...  3.96 us
  transfers between devices with their start and end apart: 2, of which 2 were waited for; matrix products, arithmetic and copies ran while one was open for 1% of the time, Pallas kernels for 0%

profile of v1, /device:TPU:0, one launch (start us, length us, event | category | flops | bytes accessed | tf_op | source)
XLA Modules:
  0.0 187.1 jit_solution(15174318598986705421)
XLA Ops:
  1.5 1.5 fusion.165
  3.1 1.5 fusion.167
  4.9 1.2 fusion.135
  6.1 11.6 %all-gather = bf16[2432,128]{1,0:T(8,128)(2,1)S(1)} all-gather(bf16[304,128]{1,0:T(8,128)(2,1)S(1)} %pad_maximum_fusion.26), channel_id=2, replica_groups=mesh['tm'=8,'batch'=4] {'tm'}, dimensions={0}, use_global_device_ids=true | all-gather | bytes 700416 | tf_op jit(solution)/shard_map/all_gather | solution.py:157
  19.6 0.8 copy-done.26
  20.4 0.9 fusion.76
  21.7 0.9 fusion.75
  23.0 0.9 fusion.74
  25.6 0.8 fusion.20
  27.4 0.8 copy-done.29
  28.2 0.9 fusion.73
  29.5 0.9 fusion.72
  30.8 0.9 fusion.71
  33.4 2.4 %fusion.48 = f32[128,128]{1,0:T(8,128)S(1)} fusion(f32[128,128]{1,0:T(8,128)S(1)} %fusion.20, bf16[128,5120]{1,0:T(8,128)(2,1)} %param.32, f32[128]{0:T(128)S(1)} %broadcast_multiply_fusion, f32[128,128]{0,1:T(8,128)S(1)} %copy.85), kind=kOutput, calls=%fused_computation.83 | convolution fusion | flops 170442752 | bytes 1507840 | tf_op jit(solution)/shard_map/dot_general | solution.py:30
  38.9 1.1 copy-done.5
  41.2 9.4 %all-gather.2 = f32[8,4,1024]{2,1,0:T(4,128)S(1)} all-gather(f32[1,4,1024]{2,1,0:T(4,128)S(1)} %maximum_bitcast_fusion), channel_id=3, replica_groups=mesh['tm'=8,'batch'=4] {'tm'}, dimensions={0}, use_global_device_ids=true | all-gather | bytes 147456 | tf_op jit(solution)/shard_map/all_gather | solution.py:192
  51.2 0.9 fusion.163
  53.7 0.8 broadcast_compare_fusion.3
  54.5 0.8 broadcast_compare_fusion.2
  55.3 1.3 fusion.93
  63.2 1.0 copy-done.10
  69.5 3.4 %all-to-all-start = ((bf16[8,128,128]{2,1,0:T(8,128)(2,1)}), bf16[8,128,128]{2,1,0:T(8,128)(2,1)S(1)}, u32[]{:S(2)}, u32[]{:S(2)}) async-start(bf16[8,128,128]{2,1,0:T(8,128)(2,1)} %pad_maximum_fusion.20), calls=%async_computation | async-start | bytes 524288 | tf_op jit(solution)/shard_map/all_to_all | solution.py:229
  73.0 1.8 fusion.195
  75.7 4.1 %all-to-all-done = bf16[8,128,128]{2,1,0:T(8,128)(2,1)S(1)} async-done(((bf16[8,128,128]{2,1,0:T(8,128)(2,1)}), bf16[8,128,128]{2,1,0:T(8,128)(2,1)S(1)}, u32[]{:S(2)}, u32[]{:S(2)}) %all-to-all-start) | async-done | bytes 262176 | tf_op jit(solution)/shard_map/all_to_all | solution.py:229
  84.4 0.9 pad_maximum_fusion.10
  85.3 4.0 %all-to-all-start.1 = ((bf16[32,96,128]{2,1,0:T(8,128)(2,1)}), bf16[32,96,128]{2,1,0:T(8,128)(2,1)S(1)}, u32[]{:S(2)}, u32[]{:S(2)}) async-start(bf16[32,96,128]{2,1,0:T(8,128)(2,1)} %pad_maximum_fusion.10), calls=%async_computation.1 | async-start | bytes 1572864 | tf_op jit(solution)/shard_map/all_to_all | solution.py:254
  89.3 19.5 %all-to-all-done.1 = bf16[32,96,128]{2,1,0:T(8,128)(2,1)S(1)} async-done(((bf16[32,96,128]{2,1,0:T(8,128)(2,1)}), bf16[32,96,128]{2,1,0:T(8,128)(2,1)S(1)}, u32[]{:S(2)}, u32[]{:S(2)}) %all-to-all-start.1) | async-done | bytes 786464 | tf_op jit(solution)/shard_map/all_to_all | solution.py:254
  109.0 1.2 copy-done.7
  110.8 1.5 fusion.26
  112.3 71.9 %all_gather.19 = bf16[2560,128]{1,0:T(8,128)(2,1)S(1)} all-gather(bf16[80,128]{1,0:T(8,128)(2,1)S(1)} %fusion.26), channel_id=1, replica_groups=mesh['tm'=8,'batch'=4] {'tm','batch'}, dimensions={0}, use_global_device_ids=true | all-gather | bytes 675840 | tf_op jit(solution)/shard_map/all_gather | solution.py:264
  184.2 1.1 copy_bitcast_fusion
  185.9 1.2 divide_bitcast_fusion
  (182 shorter events, 29.4 us)
Async XLA Ops:
  0.6 4.2 %copy-start = (bf16[1,128,5120]{2,1,0:T(8,128)(2,1)S(1)}, bf16[1,128,5120]{2,1,0:T(8,128)(2,1)}, u32[]{:S(2)}) copy-start(bf16[1,128,5120]{2,1,0:T(8,128)(2,1)} %param.20) | copy-start | bytes 3932164
  0.6 4.2 %copy-start.8 = (bf16[64,5120]{1,0:T(8,128)(2,1)S(1)}, bf16[64,5120]{1,0:T(8,128)(2,1)}, u32[]{:S(2)}) copy-start(bf16[64,5120]{1,0:T(8,128)(2,1)} %param.21) | copy-start | bytes 1966084
  0.7 4.2 %copy-start.23 = (bf16[1,64,128]{2,1,0:T(8,128)(2,1)S(1)}, bf16[1,64,128]{2,1,0:T(8,128)(2,1)}, u32[]{:S(2)}) copy-start(bf16[1,64,128]{2,1,0:T(8,128)(2,1)} %param.22) | copy-start | bytes 49156
  4.9 13.5 %copy-start.1 = (bf16[128,5120]{1,0:T(8,128)(2,1)S(1)}, bf16[128,5120]{1,0:T(8,128)(2,1)}, u32[]{:S(2)}) copy-start(bf16[128,5120]{1,0:T(8,128)(2,1)} %param.24) | copy-start | bytes 3932164
  19.1 1.3 copy-start.26
  20.4 1.3 copy-start.27
  21.3 1.3 copy-start.12
  21.7 1.3 copy-start.28
  22.7 1.3 copy-start.13
  24.0 1.3 copy-start.2
  26.9 1.3 copy-start.29
  28.2 1.3 copy-start.30
  29.1 1.3 copy-start.15
  29.5 1.3 copy-start.31
  30.5 1.3 copy-start.16
  31.8 1.4 copy-start.17
  33.4 2.5 %slice-start = ((f32[144,128]{1,0:T(8,128)}), f32[128,128]{1,0:T(8,128)S(1)}, s32[]{:S(2)}) async-start(f32[144,128]{1,0:T(8,128)} %copy-done.12), calls=%async_computation.2 | async-start | bytes 131072 | tf_op jit(solution)/shard_map/slice | solution.py:55
  33.4 2.5 %slice-start.1 = ((f32[144,128]{1,0:T(8,128)}), f32[128,128]{1,0:T(8,128)S(1)}, s32[]{:S(2)}) async-start(f32[144,128]{1,0:T(8,128)} %copy-done.13), calls=%async_computation.3 | async-start | bytes 131072 | tf_op jit(solution)/shard_map/slice | solution.py:55
  33.4 2.5 %slice-start.2 = ((f32[144,128]{1,0:T(8,128)}), f32[128,128]{1,0:T(8,128)S(1)}, s32[]{:S(2)}) async-start(f32[144,128]{1,0:T(8,128)} %copy-done.14), calls=%async_computation.4 | async-start | bytes 131072 | tf_op jit(solution)/shard_map/slice | solution.py:55
  37.7 1.1 copy-start.4
  38.8 1.2 copy-start.5
  38.8 1.2 copy-start.19
  51.2 5.4 %copy-start.6 = (f32[1024,384]{0,1:T(8,128)S(1)}, f32[1024,384]{0,1:T(8,128)}, u32[]{:S(2)}) copy-start(f32[1024,384]{0,1:T(8,128)} %copy-done.5) | copy-start | bytes 4718596
  63.1 1.1 copy-start.10
  63.1 1.5 copy-start.32
  65.2 1.5 copy-start.33
  69.5 10.3 %all-to-all-start = ((bf16[8,128,128]{2,1,0:T(8,128)(2,1)}), bf16[8,128,128]{2,1,0:T(8,128)(2,1)S(1)}, u32[]{:S(2)}, u32[]{:S(2)}) async-start(bf16[8,128,128]{2,1,0:T(8,128)(2,1)} %pad_maximum_fusion.20), calls=%async_computation | async-start | bytes 524288 | tf_op jit(solution)/shard_map/all_to_all | solution.py:229
  72.9 1.8 copy-start.3
  72.9 1.8 copy-start.11
  74.8 5.0 %copy-start.18 = (f32[64,128]{1,0:T(8,128)S(1)}, f32[64,128]{1,0:T(8,128)}, u32[]{:S(2)}) copy-start(f32[64,128]{1,0:T(8,128)} %get-tuple-element.45) | copy-start | bytes 98308
  85.3 23.5 %all-to-all-start.1 = ((bf16[32,96,128]{2,1,0:T(8,128)(2,1)}), bf16[32,96,128]{2,1,0:T(8,128)(2,1)S(1)}, u32[]{:S(2)}, u32[]{:S(2)}) async-start(bf16[32,96,128]{2,1,0:T(8,128)(2,1)} %pad_maximum_fusion.10), calls=%async_computation.1 | async-start | bytes 1572864 | tf_op jit(solution)/shard_map/all_to_all | solution.py:254
  108.9 1.2 copy-start.7
  (10 other events, 8.7 us)

commit v2 on v1

--- a/solution.py
+++ b/solution.py
@@ -242,32 +242,30 @@
     gap_diff = -noise_level * velocity_diff
     difference = gap_diff.astype(jnp.bfloat16)
     partial_grad = jnp.dot(difference, hidden_states[0], preferred_element_type=jnp.float32)
-    everyone = devices * samples
     lanes = 128
     blocks = jnp.transpose(
         partial_grad.astype(jnp.bfloat16).reshape(patch_rows, width // lanes, lanes), (1, 0, 2)
-    ).reshape(everyone, -1, lanes)
+    ).reshape(devices, -1, lanes)
     chunk_rows = blocks.shape[1]
     gap_top, gap_low = split_two(gap_local)
-    lane = lax.broadcasted_iota(jnp.int32, (everyone, 16, lanes), 2)
+    lane = lax.broadcasted_iota(jnp.int32, (devices, 16, lanes), 2)
     gap_rows = jnp.where(lane == 0, gap_top, gap_low)
     traded = lax.all_to_all(
-        jnp.concatenate([blocks, gap_rows], axis=1), ("tm", "batch"), 0, 0, tiled=True
+        jnp.concatenate([blocks, gap_rows], axis=1), "tm", 0, 0, tiled=True
     ).astype(jnp.float32)
-    gaps = traded[:, chunk_rows, 0] + traded[:, chunk_rows, 1]
-    gap_total = jnp.sum(gaps.reshape(devices, samples), axis=0)
+    gap_total = jnp.sum(traded[:, chunk_rows, 0] + traded[:, chunk_rows, 1])
     count_all = patch_rows * tokens
-    normalizers = jnp.maximum(gap_total / count_all, gap_floor)
+    own_norm = jnp.maximum(gap_total / count_all, gap_floor)
     grad_root = math.sqrt(samples * hidden_states.shape[0] * tokens)
-    per_source = jnp.tile(1.0 / (normalizers * grad_root), devices)
-    own_chunk = jnp.sum(traded[:, :chunk_rows] * per_source[:, None, None], axis=0)
-    whole = lax.all_gather(own_chunk.astype(jnp.bfloat16), ("tm", "batch"), axis=0, tiled=True)
+    sample_chunk = jnp.sum(traded[:, :chunk_rows], axis=0) / own_norm / grad_root
+    sample_chunks = lax.all_gather(sample_chunk.astype(jnp.bfloat16), "batch", axis=0, tiled=False)
+    own_chunk = jnp.sum(sample_chunks.astype(jnp.float32), axis=0)
+    whole = lax.all_gather(own_chunk.astype(jnp.bfloat16), "tm", axis=0, tiled=True)
     weight_grad = (
         jnp.transpose(whole.reshape(width // lanes, patch_rows, lanes), (1, 0, 2))
         .reshape(patch_rows, width)
         .astype(jnp.float32)
     )
-    own_norm = lax.dynamic_index_in_dim(normalizers, lax.axis_index("batch"), 0, keepdims=False)
     dmd_gradient = (gap_diff / own_norm)[None]
     return (dmd_gradient, weight_grad)
 

time: 188 us -> 126 us (0.67)
  blocking collectives: 92.8 us -> 58.5 us
  waiting for transfers between devices: 23.6 us -> 4.12 us
  starting transfers between devices: 7.37 us -> 3.41 us
  other arithmetic: 17.4 us -> 14.7 us
  local copies, waits for them, and re-layouts: 14 us -> 12 us
    all_gather x1 -> x2, blocking collectives: 71.9 us -> 23.7 us  [the longest x1 14.3 us: per_device(): lax.all_gather(sample_chunk.astype(jnp.bfloat16), 'batch', axis=0, tiled=...]
    all_to_all x1 -> x0, waiting for transfers between devices: 19.5 us -> none  [per_device(): lax.all_to_all(jnp.concatenate([blocks, gap_rows], axis=1), ('tm', 'batch...]
    all_to_all x0 -> x1, blocking collectives: none -> 13.9 us  [per_device(): lax.all_to_all(jnp.concatenate([blocks, gap_rows], axis=1), 'tm', 0, 0, t...]
    all_to_all x1 -> x0, starting transfers between devices: 3.96 us -> none  [per_device(): lax.all_to_all(jnp.concatenate([blocks, gap_rows], axis=1), ('tm', 'batch...]
    unnamed x68 -> x66, local copies, waits for them, and re-layouts: 9.39 us -> 8.19 us
  transfers between devices with their start and end apart: 2 -> 1, of which waited for: 2 -> 1; matrix products, arithmetic and copies ran while one was open for 1% -> 2% of each run, Pallas kernels for 0% -> 0%
where the time goes in v2:
time: 126 us; the launch traced here: 125 us
  blocking collectives  58.5 us (46%)
  matrix products  26.3 us (21%)
  other arithmetic  14.7 us (12%)
  local copies, waits for them, and re-layouts  12 us (10%)
  between operations  6.29 us (5%)
  waiting for transfers between devices  4.12 us (3%)
  starting transfers between devices  3.41 us (3%)
    dot_general x23, matrix products, dot32(): lax.dot_general(left, right, (((left_dim,), (right_dim,)), ((), ())), pre...  18.2 us
    all_gather x1, blocking collectives, per_device(): lax.all_gather(sample_chunk.astype(jnp.bfloat16), 'batch', axis=0, tiled=...  14.3 us
    all_to_all x1, blocking collectives, per_device(): lax.all_to_all(jnp.concatenate([blocks, gap_rows], axis=1), 'tm', 0, 0, t...  13.9 us
    all_gather x1, blocking collectives, per_device(): gathered = lax.all_gather(payload, 'tm', axis=0, tiled=False)  11.6 us
    all_gather x1, blocking collectives, per_device(): lax.all_gather(own_chunk.astype(jnp.bfloat16), 'tm', axis=0, tiled=True)  9.38 us
    all_gather x1, blocking collectives, per_device(): lax.all_gather(squares, 'tm', axis=0, tiled=False)  9.36 us
    unnamed x66, local copies, waits for them, and re-layouts  8.19 us
    all_to_all x1, waiting for transfers between devices, per_device(): landed = lax.all_to_all(sent, 'tm', 0, 0, tiled=True)  4.12 us
  transfers between devices with their start and end apart: 1, of which 1 were waited for; matrix products, arithmetic and copies ran while one was open for 2% of the time, Pallas kernels for 0%

profile of v2, /device:TPU:0, one launch (start us, length us, event | category | flops | bytes accessed | tf_op | source)
XLA Modules:
  0.0 125.3 jit_solution(5180608725157418603)
XLA Ops:
  1.5 1.5 %fusion.164 = bf16[1,3,5120]{2,0,1:T(2,128)(2,1)S(1)} fusion(bf16[32,3,5120]{2,0,1:T(8,128)(2,1)} %param.33, bf16[256]{0:T(256)(128)(2,1)S(1)} %pad_maximum_fusion.29, s32[]{:T(128)S(6)} %select_n.43), kind=kOutput, calls=%fused_computation.288 | convolution fusion | flops 983040 | bytes 1014276 | tf_op jit(solution)/shard_map/f,fcd->cd/dot_general | solution.py:151
  3.1 1.5 %fusion.166 = bf16[1,3,5120]{2,0,1:T(2,128)(2,1)S(1)} fusion(bf16[32,3,5120]{2,0,1:T(8,128)(2,1)} %param.25, bf16[256]{0:T(256)(128)(2,1)S(1)} %pad_maximum_fusion.29, s32[]{:T(128)S(6)} %select_n.43), kind=kOutput, calls=%fused_computation.290 | convolution fusion | flops 983040 | bytes 1014276 | tf_op jit(solution)/shard_map/f,fcd->cd/dot_general | solution.py:151
  4.9 1.2 fusion.134
  6.1 11.6 %all-gather = bf16[2432,128]{1,0:T(8,128)(2,1)S(1)} all-gather(bf16[304,128]{1,0:T(8,128)(2,1)S(1)} %pad_maximum_fusion.26), channel_id=2, replica_groups=mesh['tm'=8,'batch'=4] {'tm'}, dimensions={0}, use_global_device_ids=true | all-gather | bytes 700416 | tf_op jit(solution)/shard_map/all_gather | solution.py:157
  19.6 0.8 copy-done.25
  20.4 0.9 fusion.75
  21.7 0.9 fusion.74
  23.0 0.9 fusion.73
  24.0 0.8 fusion.22
  25.6 0.8 fusion.20
  27.4 0.8 copy-done.28
  28.2 0.9 fusion.72
  29.5 0.9 fusion.71
  30.8 0.9 fusion.70
  33.4 2.4 %fusion.47 = f32[128,128]{1,0:T(8,128)S(1)} fusion(f32[128,128]{1,0:T(8,128)S(1)} %fusion.20, bf16[128,5120]{1,0:T(8,128)(2,1)} %param.32, f32[128]{0:T(128)S(1)} %broadcast_multiply_fusion, f32[128,128]{0,1:T(8,128)S(1)} %copy.106), kind=kOutput, calls=%fused_computation.82 | convolution fusion | flops 170442752 | bytes 1507840 | tf_op jit(solution)/shard_map/dot_general | solution.py:30
  38.1 0.8 copy-done.4
  38.9 1.1 copy-done.5
  41.2 9.4 %all-gather.3 = f32[8,4,1024]{2,1,0:T(4,128)S(1)} all-gather(f32[1,4,1024]{2,1,0:T(4,128)S(1)} %maximum_bitcast_fusion), channel_id=3, replica_groups=mesh['tm'=8,'batch'=4] {'tm'}, dimensions={0}, use_global_device_ids=true | all-gather | bytes 147456 | tf_op jit(solution)/shard_map/all_gather | solution.py:192
  51.2 0.9 fusion.161
  52.1 0.8 slice_bitcast_fusion.16
  52.9 0.8 slice_bitcast_fusion.15
  53.7 0.8 broadcast_compare_fusion.3
  54.5 0.8 broadcast_compare_fusion.2
  55.3 1.3 %fusion.92 = (bf16[1,1024,128]{1,2,0:T(8,128)(2,1)S(1)}, bf16[1,1024,128]{1,2,0:T(8,128)(2,1)S(1)}) fusion(f32[1024,384]{0,1:T(8,128)} %copy-done.4, f32[128]{0:T(128)S(1)} %get-tuple-element.38, f32[1024]{0:T(1024)S(1)} %bitcast.188, f32[128]{0:T(128)S(1)} %get-tuple-element.39, f32[1024]{0:T(1024)S(1)} %bitcast.189), kind=kLoop, calls=%fused_computation.165 | loop fusion | flops 786432 | bytes 1582080 | tf_op jit(solution)/shard_map/stack | solution.py:203
  63.2 1.0 copy-done.9
  69.5 3.4 %all-to-all-start = ((bf16[8,128,128]{2,1,0:T(8,128)(2,1)}), bf16[8,128,128]{2,1,0:T(8,128)(2,1)S(1)}, u32[]{:S(2)}, u32[]{:S(2)}) async-start(bf16[8,128,128]{2,1,0:T(8,128)(2,1)} %pad_maximum_fusion.20), calls=%async_computation | async-start | bytes 524288 | tf_op jit(solution)/shard_map/all_to_all | solution.py:229
  72.9 1.8 %fusion.194 = f32[64,128]{1,0:T(8,128)S(1)} fusion(bf16[64,5120]{1,0:T(8,128)(2,1)} %param.31, bf16[128,5120]{1,0:T(8,128)(2,1)S(1)} %copy-done.1), kind=kOutput, calls=%fused_computation.327 | convolution fusion | flops 83886080 | bytes 1998848 | tf_op jit(solution)/shard_map/dot_general | solution.py:30
  75.6 4.1 %all-to-all-done = bf16[8,128,128]{2,1,0:T(8,128)(2,1)S(1)} async-done(((bf16[8,128,128]{2,1,0:T(8,128)(2,1)}), bf16[8,128,128]{2,1,0:T(8,128)(2,1)S(1)}, u32[]{:S(2)}, u32[]{:S(2)}) %all-to-all-start) | async-done | bytes 262176 | tf_op jit(solution)/shard_map/all_to_all | solution.py:229
  84.4 13.9 %all_to_all.10 = bf16[8,336,128]{2,1,0:T(8,128)(2,1)S(1)} all-to-all(bf16[8,336,128]{2,1,0:T(8,128)(2,1)S(1)} %pad_maximum_fusion.10), channel_id=1, replica_groups=mesh['tm'=8,'batch'=4] {'tm'}, dimensions={0} | all-to-all | bytes 1376256 | tf_op jit(solution)/shard_map/all_to_all | solution.py:253
  100.4 14.3 %all-gather.2 = bf16[1280,128]{1,0:T(8,128)(2,1)S(1)} all-gather(bf16[320,128]{1,0:T(8,128)(2,1)S(1)} %multiply_convert_fusion.4), channel_id=4, replica_groups=mesh['tm'=8,'batch'=4] {'batch'}, dimensions={0}, use_global_device_ids=true | all-gather | bytes 409600 | tf_op jit(solution)/shard_map/all_gather | solution.py:261
  114.8 9.4 %all_gather.24 = bf16[2560,128]{1,0:T(8,128)(2,1)S(1)} all-gather(bf16[320,128]{1,0:T(8,128)(2,1)S(1)} %reduce_sum.192), channel_id=1, replica_groups=mesh['tm'=8,'batch'=4] {'tm'}, dimensions={0}, use_global_device_ids=true | all-gather | bytes 737280 | tf_op jit(solution)/shard_map/all_gather | solution.py:263
  124.2 1.1 copy_bitcast_fusion
  (176 shorter events, 26.4 us)
Async XLA Ops:
  0.6 4.2 %copy-start = (bf16[1,128,5120]{2,1,0:T(8,128)(2,1)S(1)}, bf16[1,128,5120]{2,1,0:T(8,128)(2,1)}, u32[]{:S(2)}) copy-start(bf16[1,128,5120]{2,1,0:T(8,128)(2,1)} %param.20) | copy-start | bytes 3932164
  0.6 4.2 %copy-start.7 = (bf16[64,5120]{1,0:T(8,128)(2,1)S(1)}, bf16[64,5120]{1,0:T(8,128)(2,1)}, u32[]{:S(2)}) copy-start(bf16[64,5120]{1,0:T(8,128)(2,1)} %param.21) | copy-start | bytes 1966084
  0.7 4.2 %copy-start.22 = (bf16[1,64,128]{2,1,0:T(8,128)(2,1)S(1)}, bf16[1,64,128]{2,1,0:T(8,128)(2,1)}, u32[]{:S(2)}) copy-start(bf16[1,64,128]{2,1,0:T(8,128)(2,1)} %param.22) | copy-start | bytes 49156
  4.9 13.5 %copy-start.1 = (bf16[128,5120]{1,0:T(8,128)(2,1)S(1)}, bf16[128,5120]{1,0:T(8,128)(2,1)}, u32[]{:S(2)}) copy-start(bf16[128,5120]{1,0:T(8,128)(2,1)} %param.24) | copy-start | bytes 3932164
  19.1 1.3 %copy-start.25 = (bf16[5120,128]{1,0:T(8,128)(2,1)S(1)}, bf16[5120,128]{1,0:T(8,128)(2,1)}, u32[]{:S(2)}) copy-start(bf16[5120,128]{1,0:T(8,128)(2,1)} %param.26) | copy-start | bytes 3932164
  20.4 1.3 %copy-start.26 = (bf16[5120,128]{1,0:T(8,128)(2,1)S(1)}, bf16[5120,128]{1,0:T(8,128)(2,1)}, u32[]{:S(2)}) copy-start(bf16[5120,128]{1,0:T(8,128)(2,1)} %param.27) | copy-start | bytes 3932164
  21.3 1.3 %copy-start.11 = (f32[144,128]{1,0:T(8,128)}, f32[144,128]{1,0:T(8,128)S(1)}, u32[]{:S(2)}) copy-start(f32[144,128]{1,0:T(8,128)S(1)} %slice_add_fusion.5) | copy-start | bytes 221188
  21.7 1.3 %copy-start.27 = (bf16[5120,128]{1,0:T(8,128)(2,1)S(1)}, bf16[5120,128]{1,0:T(8,128)(2,1)}, u32[]{:S(2)}) copy-start(bf16[5120,128]{1,0:T(8,128)(2,1)} %param.28) | copy-start | bytes 3932164
  22.7 1.3 %copy-start.12 = (f32[144,128]{1,0:T(8,128)}, f32[144,128]{1,0:T(8,128)S(1)}, u32[]{:S(2)}) copy-start(f32[144,128]{1,0:T(8,128)S(1)} %slice_add_fusion.4) | copy-start | bytes 221188
  24.0 1.3 %copy-start.2 = (bf16[128,5120]{1,0:T(8,128)(2,1)S(1)}, bf16[128,5120]{1,0:T(8,128)(2,1)}, u32[]{:S(2)}) copy-start(bf16[128,5120]{1,0:T(8,128)(2,1)} %param.32) | copy-start | bytes 3932164
  26.9 1.3 %copy-start.28 = (bf16[5120,128]{1,0:T(8,128)(2,1)S(1)}, bf16[5120,128]{1,0:T(8,128)(2,1)}, u32[]{:S(2)}) copy-start(bf16[5120,128]{1,0:T(8,128)(2,1)} %param.34) | copy-start | bytes 3932164
  28.2 1.3 %copy-start.29 = (bf16[5120,128]{1,0:T(8,128)(2,1)S(1)}, bf16[5120,128]{1,0:T(8,128)(2,1)}, u32[]{:S(2)}) copy-start(bf16[5120,128]{1,0:T(8,128)(2,1)} %param.35) | copy-start | bytes 3932164
  29.2 1.3 %copy-start.14 = (f32[144,128]{1,0:T(8,128)}, f32[144,128]{1,0:T(8,128)S(1)}, u32[]{:S(2)}) copy-start(f32[144,128]{1,0:T(8,128)S(1)} %slice_add_fusion.2) | copy-start | bytes 221188
  29.5 1.3 %copy-start.30 = (bf16[5120,128]{1,0:T(8,128)(2,1)S(1)}, bf16[5120,128]{1,0:T(8,128)(2,1)}, u32[]{:S(2)}) copy-start(bf16[5120,128]{1,0:T(8,128)(2,1)} %param.36) | copy-start | bytes 3932164
  30.5 1.3 %copy-start.15 = (f32[144,128]{1,0:T(8,128)}, f32[144,128]{1,0:T(8,128)S(1)}, u32[]{:S(2)}) copy-start(f32[144,128]{1,0:T(8,128)S(1)} %slice_add_fusion.1) | copy-start | bytes 221188
  31.8 1.4 %copy-start.16 = (f32[144,128]{1,0:T(8,128)}, f32[144,128]{1,0:T(8,128)S(1)}, u32[]{:S(2)}) copy-start(f32[144,128]{1,0:T(8,128)S(1)} %slice_add_fusion) | copy-start | bytes 221188
  33.4 2.5 %slice-start = ((f32[144,128]{1,0:T(8,128)}), f32[128,128]{1,0:T(8,128)S(1)}, s32[]{:S(2)}) async-start(f32[144,128]{1,0:T(8,128)} %copy-done.11), calls=%async_computation.2 | async-start | bytes 131072 | tf_op jit(solution)/shard_map/slice | solution.py:55
  33.4 2.5 %slice-start.1 = ((f32[144,128]{1,0:T(8,128)}), f32[128,128]{1,0:T(8,128)S(1)}, s32[]{:S(2)}) async-start(f32[144,128]{1,0:T(8,128)} %copy-done.12), calls=%async_computation.3 | async-start | bytes 131072 | tf_op jit(solution)/shard_map/slice | solution.py:55
  33.4 2.5 %slice-start.2 = ((f32[144,128]{1,0:T(8,128)}), f32[128,128]{1,0:T(8,128)S(1)}, s32[]{:S(2)}) async-start(f32[144,128]{1,0:T(8,128)} %copy-done.13), calls=%async_computation.4 | async-start | bytes 131072 | tf_op jit(solution)/shard_map/slice | solution.py:55
  37.7 1.1 copy-start.4
  38.8 1.2 copy-start.5
  38.8 1.2 copy-start.18
  51.2 5.4 %copy-start.6 = (f32[1024,384]{0,1:T(8,128)S(1)}, f32[1024,384]{0,1:T(8,128)}, u32[]{:S(2)}) copy-start(f32[1024,384]{0,1:T(8,128)} %copy-done.5) | copy-start | bytes 4718596
  63.0 1.1 copy-start.9
  63.0 1.1 copy-start.21
  63.1 1.5 %copy-start.31 = (bf16[128,5120]{1,0:T(8,128)(2,1)S(1)}, bf16[128,5120]{1,0:T(8,128)(2,1)}, u32[]{:S(2)}) copy-start(bf16[128,5120]{1,0:T(8,128)(2,1)} %param.37) | copy-start | bytes 3932164
  65.2 1.1 copy-start.8
  65.2 1.5 %copy-start.32 = (bf16[128,5120]{1,0:T(8,128)(2,1)S(1)}, bf16[128,5120]{1,0:T(8,128)(2,1)}, u32[]{:S(2)}) copy-start(bf16[128,5120]{1,0:T(8,128)(2,1)} %param.29) | copy-start | bytes 3932164
  69.5 10.3 %all-to-all-start = ((bf16[8,128,128]{2,1,0:T(8,128)(2,1)}), bf16[8,128,128]{2,1,0:T(8,128)(2,1)S(1)}, u32[]{:S(2)}, u32[]{:S(2)}) async-start(bf16[8,128,128]{2,1,0:T(8,128)(2,1)} %pad_maximum_fusion.20), calls=%async_computation | async-start | bytes 524288 | tf_op jit(solution)/shard_map/all_to_all | solution.py:229
  72.9 1.8 %copy-start.3 = (bf16[128,5120]{1,0:T(8,128)(2,1)S(1)}, bf16[128,5120]{1,0:T(8,128)(2,1)}, u32[]{:S(2)}) copy-start(bf16[128,5120]{1,0:T(8,128)(2,1)} %param.32) | copy-start | bytes 3932164
  72.9 1.8 %copy-start.10 = (bf16[64,5120]{1,0:T(8,128)(2,1)S(1)}, bf16[64,5120]{1,0:T(8,128)(2,1)}, u32[]{:S(2)}) copy-start(bf16[64,5120]{1,0:T(8,128)(2,1)} %param.39) | copy-start | bytes 1966084
  74.8 5.0 %copy-start.17 = (f32[64,128]{1,0:T(8,128)S(1)}, f32[64,128]{1,0:T(8,128)}, u32[]{:S(2)}) copy-start(f32[64,128]{1,0:T(8,128)} %get-tuple-element.43) | copy-start | bytes 98308
  (8 other events, 6.5 us)
